TPU v7x, 512 devices: a whole 4x8x8 slice. The times are simulated.
512 devices in a mesh: segment: 2 (over core), dp: 64 (over y, z), rows: 4 (over x).
Axes of the slice: x: 4, y: 8, z: 8, core: 2. Of those that a mesh axis runs over, the one named last changes fastest.
Arguments:
- latent: bfloat16 [128, 16, 16, 320], P('dp', 'rows'), may hold values from -6 to 6
- hint: bfloat16 [128, 16, 16, 320], P('dp', 'rows'), may hold values from -6 to 6
- decoder_in: bfloat16 [128, 16, 16, 320], P('dp', 'rows'), may hold values from -6 to 6
- target: bfloat16 [128, 16, 16, 320], P('dp', 'rows'), may hold values from -6 to 6
- first_convs: bfloat16 [2, 2, 2880, 320], P('segment', None, 'dp'), may hold values from -0.109375 to 0.109375
- second_convs: bfloat16 [2, 2880, 320], P('segment', 'dp'), may hold values from -0.109375 to 0.109375
- pointwise_weights: bfloat16 [2, 2, 320, 320], P('segment', None, 'dp'), may hold values from -0.3125 to 0.3125
Outputs:
- grad_first: float32 [921600], P(('segment', 'dp', 'rows'))
- grad_zero: float32 [102400], P(('segment', 'dp', 'rows'))
All inputs are finite; a program needn't handle non-finite values.
Results may differ from a plain program's by a relative error of at most 0.0095.
Values may be sent and summed in bfloat16 or wider, within the bound.
A program may use at most 64 MiB of HBM per device.

v0:
```python
import math

import jax
import jax.numpy as jnp
from jax import lax
from jax.sharding import PartitionSpec as P


def padded_2(block, sides, width):
    for axis, dim in sides:
        count = lax.axis_size(axis)
        forward = [(i, i + 1) for i in range(count - 1)]
        backward = [(target, source) for source, target in forward]
        low = lax.ppermute(
            lax.slice_in_dim(block, block.shape[dim] - width, None, axis=dim), axis, forward
        )
        high = lax.ppermute(lax.slice_in_dim(block, 0, width, axis=dim), axis, backward)
        block = jnp.concatenate([low, block, high], axis=dim)
    return block


def shifted(array, axis, by):
    count = lax.axis_size(axis)
    pairs = [(i, i + by) for i in range(count) if 0 <= i + by < count]
    return lax.ppermute(array, axis, pairs)


def swish_slope(value):
    logistic = jax.nn.sigmoid(value)
    return logistic * (1.0 + value * (1.0 - logistic))


def conv_rows(padded, weight):
    kernel = weight.reshape(3, 3, weight.shape[0] // 9, weight.shape[1])
    return lax.conv_general_dilated(
        padded,
        kernel,
        (1, 1),
        ((0, 0), (1, 1)),
        dimension_numbers=("NHWC", "HWIO", "NHWC"),
        preferred_element_type=jnp.float32,
    )


def kernel_grad(padded, cotangent):
    result = lax.conv_general_dilated(
        padded,
        cotangent,
        (1, 1),
        ((0, 0), (1, 1)),
        dimension_numbers=("CHWN", "IHWO", "HWNC"),
        preferred_element_type=jnp.float32,
    )
    return result.reshape(-1, result.shape[-1])


def project(values, weight):
    flat = values.reshape(-1, values.shape[-1])
    return jnp.dot(flat, weight, preferred_element_type=jnp.float32).reshape(
        values.shape[:-1] + (weight.shape[1],)
    )


def flipped(weight, channels):
    grid = weight.reshape(3, 3, channels, channels)[::-1, ::-1]
    return jnp.swapaxes(grid, 2, 3).reshape(9 * channels, channels)


def contract_rows(left, right):
    return lax.dot_general(
        left, right, (((0,), (0,)), ((), ())), preferred_element_type=jnp.float32
    )


def per_device(latent, hint, decoder_in, target, first_convs, second_convs, pointwise_weights):
    samples, height, width, channels = latent.shape
    first_all, point_all = (
        lax.all_gather(first_convs, "dp", axis=2, tiled=True),
        lax.all_gather(pointwise_weights, "dp", axis=2, tiled=True),
    )
    second_all = lax.all_gather(second_convs, "dp", axis=1, tiled=True)
    first_left = first_all[0, 0]
    first_right = first_all[0, 1]
    second_main = second_all[0]
    second_back = flipped(second_main, channels)
    point_left = point_all[0, 0]
    point_right = point_all[0, 1]
    right_back = point_right.T
    segment_zero = lax.axis_index("segment") == 0
    scale = 1.0 / math.sqrt(samples * lax.axis_size("dp") * height * lax.axis_size("rows") * width)
    blocks = 1
    block = samples // blocks
    plane = (block, height, width, channels)
    empty = jnp.zeros(plane, jnp.bfloat16)
    received = jnp.zeros((2,) + plane, jnp.bfloat16)
    returned = empty
    error_half = empty
    dec_grad = empty
    grad_first = jnp.zeros((9 * channels, channels), jnp.float32)
    grad_zero = jnp.zeros((channels, channels), jnp.float32)
    saved = [None] * blocks
    for tick in range(blocks + 2):
        forward_zero = tick < blocks
        decode = 1 <= tick <= blocks
        backward_zero = tick >= 2
        if forward_zero or decode:
            first_index = min(tick, blocks - 1)

            def inputs_zero():
                mixed = (latent.astype(jnp.float32) + project(hint, point_left)).astype(
                    jnp.bfloat16
                )
                return jnp.stack([latent, mixed])

            def inputs_one():
                return jnp.stack([received[0], decoder_in])

            pair = lax.cond(segment_zero, inputs_zero, inputs_one)
            padded = padded_2(pair, (("rows", 2),), 1)
            out_left = conv_rows(padded[0], first_left)
            out_right = conv_rows(padded[1], first_right)

            def middle_zero():
                return jax.nn.silu(out_right).astype(jnp.bfloat16)

            def middle_one():
                return (
                    latent.astype(jnp.float32) + out_left + received[1].astype(jnp.float32)
                ).astype(jnp.bfloat16)

            middle = lax.cond(segment_zero, middle_zero, middle_one)
            padded_mid = padded_2(middle, (("rows", 1),), 1)
            out_mid = conv_rows(padded_mid, second_main)

            def finish_zero():
                enc_act = jax.nn.silu(out_left).astype(jnp.bfloat16)
                control_out = (pair[1].astype(jnp.float32) + out_mid).astype(jnp.bfloat16)
                control_proj = project(control_out, point_right).astype(jnp.bfloat16)
                return (jnp.stack([enc_act, control_proj]), control_out, empty, empty)

            def finish_one():
                dec_pre = out_right + out_mid
                output = (
                    jax.nn.silu(dec_pre)
                    + project(decoder_in, point_left)
                    + project(middle, point_right)
                )
                error = (output - target.astype(jnp.float32)) * scale
                return (
                    jnp.zeros((2,) + plane, jnp.bfloat16),
                    empty,
                    error.astype(jnp.bfloat16),
                    (error * swish_slope(dec_pre)).astype(jnp.bfloat16),
                )

            outgoing, control_out, error_half, dec_grad = lax.cond(
                segment_zero, finish_zero, finish_one
            )
            if forward_zero:
                saved[first_index] = (padded[1], out_right, control_out)
                received = shifted(outgoing, "segment", 1)
        if decode or backward_zero:
            incoming = returned

            def start_zero():
                return project(incoming, right_back).astype(jnp.bfloat16)

            def start_one():
                return dec_grad

            back = lax.cond(segment_zero, start_zero, start_one)
            padded_back = padded_2(back, (("rows", 1),), 1)
            out_back = conv_rows(padded_back, second_back)
            if backward_zero:
                held_input, held_pre, held_out = saved[tick - 2]

                def update_zero():
                    first_grad = (out_back * swish_slope(held_pre)).astype(jnp.bfloat16)
                    new_first = grad_first + kernel_grad(held_input, first_grad)
                    new_zero = grad_zero + contract_rows(
                        held_out.reshape(-1, channels), incoming.reshape(-1, channels)
                    )
                    return (new_first, new_zero, empty)

            else:

                def update_zero():
                    return (grad_first, grad_zero, empty)

            def update_one():
                skip_grad = (out_back + project(error_half, right_back)).astype(jnp.bfloat16)
                return (grad_first, grad_zero, skip_grad)

            grad_first, grad_zero, skip_grad = lax.cond(segment_zero, update_zero, update_one)
            if decode:
                returned = shifted(skip_grad, "segment", -1)
    flat_first = grad_first.reshape(-1)
    flat_zero = grad_zero.reshape(-1)
    out_first, out_zero = (
        lax.psum_scatter(flat_first, ("segment", "dp", "rows"), scatter_dimension=0, tiled=True),
        lax.psum_scatter(flat_zero, ("segment", "dp", "rows"), scatter_dimension=0, tiled=True),
    )
    return (out_first, out_zero)


def solution(mesh):
    placed = (
        P("dp", "rows", None, None),
        P("dp", "rows", None, None),
        P("dp", "rows", None, None),
        P("dp", "rows", None, None),
        P("segment", None, "dp", None),
        P("segment", "dp", None),
        P("segment", None, "dp", None),
    )
    return jax.shard_map(
        per_device,
        mesh=mesh,
        in_specs=placed,
        out_specs=(P(("segment", "dp", "rows")), P(("segment", "dp", "rows"))),
        check_vma=False,
    )
```

profile of v0, /device:TPU:1, one launch (start us, length us, event | category | flops | bytes accessed | tf_op | source)
XLA Modules:
  0.0 552.7 jit_solution(7433316878518394187)
XLA Ops:
  7.9 1.5 copy.145
  9.5 47.9 %all_gather.9 = bf16[1,2,320,320]{3,1,0,2:T(2,128)(2,1)S(1)} all-gather(bf16[1,2,5,320]{3,1,0,2:T(2,128)(2,1)} %bitcast.208), channel_id=1, replica_groups=mesh['segment'=2,'dp'=64,'rows'=4] {'dp'}, dimensions={2}, use_global_device_ids=true | all-gather | bytes 416000 | tf_op jit(solution)/shard_map/all_gather | solution.py:79
  58.3 3.1 collective-permute-start
  61.4 1.3 collective-permute-start.1
  63.1 3.3 collective-permute-done.1
  66.5 0.9 slice_bitcast_fusion.12
  67.9 31.8 %all-gather.3.cloned.1.call-done = bf16[1,2,2880,320]{3,1,0,2:T(2,128)(2,1)} async-done(((bf16[1,2,45,320]{3,1,0,2:T(2,128)(2,1)}), bf16[1,2,2880,320]{3,1,0,2:T(2,128)(2,1)}) %all-gather.3.cloned.1.call-update) | async-done | bytes 3686416 | tf_op jit(solution)/shard_map/all_gather | solution.py:78
  99.7 9.5 %fusion.71 = (bf16[1,1,2880,320]{3,1,0,2:T(2,128)(2,1)S(1)}, bf16[1,1,2880,320]{3,1,0,2:T(2,128)(2,1)S(1)}) fusion(bf16[1,2,2880,320]{3,1,0,2:T(2,128)(2,1)} %all-gather.3.cloned.1.call-done), kind=kLoop, calls=%fused_computation.126 | loop fusion | bytes 7372800 | tf_op jit(solution)/shard_map/slice | solution.py:82
  109.8 0.8 convolution_select_fusion.7
  111.4 0.8 convolution_select_fusion.6
  114.4 1.3 collective-permute-start.3
  115.6 4.6 collective-permute-start.2
  120.2 66.2 %all-gather.5.cloned.1.call-done = bf16[1,2880,320]{2,0,1:T(2,128)(2,1)} async-done(((bf16[1,45,320]{2,0,1:T(2,128)(2,1)}), bf16[1,2880,320]{2,0,1:T(2,128)(2,1)}) %all-gather.5.cloned.1.call-update) | async-done | bytes 1843216 | tf_op jit(solution)/shard_map/all_gather | solution.py:81
  186.4 2.6 copy.189
  189.1 0.8 maximum_bitcast_fusion
  190.6 0.7 convolution_select_fusion.5
  192.2 1.3 collective-permute-start.4
  193.5 7.0 %collective-permute-done.4 = bf16[2,2,4,16,320]{4,3,2,1,0:T(8,128)(2,1)} collective-permute-done((bf16[2,2,4,16,320]{4,3,2,1,0:T(8,128)(2,1)S(1)}, bf16[2,2,4,16,320]{4,3,2,1,0:T(8,128)(2,1)}, u32[]{:S(2)}, u32[]{:S(2)}) %collective-permute-start.4) | collective-permute-done | bytes 163872 | tf_op jit(solution)/shard_map/ppermute | solution.py:25
  200.5 1.0 conditional.19
  200.5 0.9 slice.48
  201.5 1.4 collective-permute-start.6
  202.9 4.2 collective-permute-start.5
  207.1 1.0 collective-permute-done.5
  208.9 0.7 convolution_select_fusion.4
  211.3 0.7 convolution_select_fusion.3
  212.2 0.9 conditional.20
  212.2 0.9 convert_add_fusion.1
  213.2 1.3 collective-permute-start.8
  214.5 4.3 collective-permute-start.7
  218.8 0.9 collective-permute-done.7
  220.5 0.7 convolution_select_fusion.2
  221.9 1.3 collective-permute-start.10
  223.2 4.3 collective-permute-start.9
  227.5 0.9 collective-permute-done.9
  229.2 1.0 convolution_select_fusion.1
  230.6 4.4 collective-permute-start.11
  235.1 0.9 collective-permute-done.11
  236.0 1.3 collective-permute-start.13
  237.3 4.6 collective-permute-start.12
  241.8 0.9 collective-permute-done.12
  243.5 1.0 convolution_select_fusion
  244.7 2.4 conditional.25
  244.7 2.3 broadcast_in_dim.13
  247.1 5.7 %reshape.49 = f32[921600]{0:T(1024)} reshape(f32[2880,320]{1,0:T(8,128)} %get-tuple-element.146) | data formatting | bytes 7372800 | tf_op jit(solution)/shard_map/reshape | solution.py:197
  252.9 1.0 reshape.50
  253.9 289.6 %all-reduce.6.cloned.1.call-done = (f32[921600]{0:T(1024)}, f32[102400]{0:T(1024)}) async-done(((f32[921600]{0:T(1024)}, f32[102400]{0:T(1024)}), (f32[921600]{0:T(1024)}, f32[102400]{0:T(1024)})) %all-reduce.6.cloned.1.call-update) | async-done | bytes 4096016
  543.5 1.4 dynamic-slice
  544.9 1.3 dynamic-slice.1
  (120 shorter events, 15.0 us)
Async XLA Ops:
  7.2 92.5 %all-gather.3.cloned.1.call-start = ((), (), s32[]{:S(2)}) async-start(), calls=%async_computation | async-start | bytes 4492800 | tf_op jit(solution)/shard_map/all_gather | solution.py:78
  7.2 50.9 %copy-start = (bf16[2,4,16,320]{3,2,1,0:T(8,128)(2,1)S(1)}, bf16[2,4,16,320]{3,2,1,0:T(8,128)(2,1)}, u32[]{:S(2)}) copy-start(bf16[2,4,16,320]{3,2,1,0:T(8,128)(2,1)} %param.27) | copy-start | bytes 245764
  7.2 50.9 %copy-start.5 = (bf16[2,4,16,320]{3,2,1,0:T(8,128)(2,1)S(1)}, bf16[2,4,16,320]{3,2,1,0:T(8,128)(2,1)}, u32[]{:S(2)}) copy-start(bf16[2,4,16,320]{3,2,1,0:T(8,128)(2,1)} %param.29) | copy-start | bytes 245764
  7.2 50.9 %copy-start.8 = (bf16[2,4,16,320]{3,2,1,0:T(8,128)(2,1)S(1)}, bf16[2,4,16,320]{3,2,1,0:T(8,128)(2,1)}, u32[]{:S(2)}) copy-start(bf16[2,4,16,320]{3,2,1,0:T(8,128)(2,1)} %param.28) | copy-start | bytes 245764
  7.9 178.5 %all-gather.5.cloned.1.call-start = ((), (), s32[]{:S(2)}) async-start(), calls=%async_computation.1 | async-start | bytes 4492800 | tf_op jit(solution)/shard_map/all_gather | solution.py:81
  9.4 534.1 %all-reduce.6.cloned.1.call-start = ((), (), s32[]{:S(2)}) async-start(), calls=%async_computation.2 | async-start | bytes 8192000
  58.3 4.5 collective-permute-start
  61.4 5.0 collective-permute-start.1
  109.1 0.7 copy-start.11
  109.5 1.4 copy-start.3
  111.4 1.4 copy-start.1
  114.4 74.7 %collective-permute-start.3 = (bf16[2,1,16,320]{3,2,1,0:T(8,128)(2,1)}, bf16[2,1,16,320]{3,2,1,0:T(8,128)(2,1)}, u32[]{:S(2)}, u32[]{:S(2)}) collective-permute-start(bf16[2,1,16,320]{3,2,1,0:T(8,128)(2,1)} %get-tuple-element.279), channel_id=1, source_target_pairs={{1,0},{2,1},{3,2},{5,4},{6,5},{7,6},{9,8},{10,9},{11,10},{13,12},{... | collective-permute-start | bytes 61448 | tf_op jit(solution)/shard_map/ppermute | solution.py:17
  115.6 73.4 %collective-permute-start.2 = (bf16[2,1,16,320]{3,2,1,0:T(8,128)(2,1)}, bf16[2,1,16,320]{3,2,1,0:T(8,128)(2,1)}, u32[]{:S(2)}, u32[]{:S(2)}) collective-permute-start(bf16[2,1,16,320]{3,2,1,0:T(8,128)(2,1)} %get-tuple-element.278), channel_id=1, source_target_pairs={{0,1},{1,2},{2,3},{4,5},{5,6},{6,7},{8,9},{9,10},{10,11},{12,13},{... | collective-permute-start | bytes 61448 | tf_op jit(solution)/shard_map/ppermute | solution.py:14
  191.4 9.1 %copy-start.6 = (bf16[2,4,16,320]{3,2,1,0:T(8,128)(2,1)S(1)}, bf16[2,4,16,320]{3,2,1,0:T(8,128)(2,1)}, u32[]{:S(2)}) copy-start(bf16[2,4,16,320]{3,2,1,0:T(8,128)(2,1)} %param.29) | copy-start | bytes 245764
  192.2 8.2 %collective-permute-start.4 = (bf16[2,2,4,16,320]{4,3,2,1,0:T(8,128)(2,1)S(1)}, bf16[2,2,4,16,320]{4,3,2,1,0:T(8,128)(2,1)}, u32[]{:S(2)}, u32[]{:S(2)}) collective-permute-start(bf16[2,2,4,16,320]{4,3,2,1,0:T(8,128)(2,1)S(1)} %get-tuple-element.142), channel_id=1, source_target_pairs={{0,256},{1,257},{2,258},{3,259},{4,260},{5,261},{6,262},{7,263},{8... | collective-permute-start | bytes 491528 | tf_op jit(solution)/shard_map/ppermute | solution.py:25
  201.4 7.5 %copy-start.4 = (bf16[1,1,2880,320]{3,2,1,0:T(8,128)(2,1)S(1)}, bf16[1,1,2880,320]{3,2,1,0:T(8,128)(2,1)}, u32[]{:S(2)}) copy-start(bf16[1,1,2880,320]{3,2,1,0:T(8,128)(2,1)} %copy-done.3) | copy-start | bytes 5529604
  201.5 5.6 %collective-permute-start.6 = (bf16[2,2,1,16,320]{4,3,2,1,0:T(8,128)(2,1)S(1)}, bf16[2,2,1,16,320]{4,3,2,1,0:T(8,128)(2,1)S(1)}, u32[]{:S(2)}, u32[]{:S(2)}) collective-permute-start(bf16[2,2,1,16,320]{4,3,2,1,0:T(8,128)(2,1)S(1)} %get-tuple-element.269), channel_id=1, source_target_pairs={{1,0},{2,1},{3,2},{5,4},{6,5},{7,6},{9,8},{10,9},{11,10},{13,12},{... | collective-permute-start | bytes 122888 | tf_op jit(solution)/shard_map/ppermute | solution.py:17
  202.9 5.2 collective-permute-start.5
  209.7 1.6 copy-start.2
  213.2 5.6 %collective-permute-start.8 = (bf16[2,1,16,320]{3,2,1,0:T(8,128)(2,1)S(1)}, bf16[2,1,16,320]{3,2,1,0:T(8,128)(2,1)S(1)}, u32[]{:S(2)}, u32[]{:S(2)}) collective-permute-start(bf16[2,1,16,320]{3,2,1,0:T(8,128)(2,1)S(1)} %get-tuple-element.277), channel_id=1, source_target_pairs={{1,0},{2,1},{3,2},{5,4},{6,5},{7,6},{9,8},{10,9},{11,10},{13,12},{... | collective-permute-start | bytes 61448 | tf_op jit(solution)/shard_map/ppermute | solution.py:17
  214.5 5.2 collective-permute-start.7
  220.5 0.9 copy-start.7
  220.5 0.9 copy-start.10
  221.9 5.6 %collective-permute-start.10 = (bf16[2,1,16,320]{3,2,1,0:T(8,128)(2,1)S(1)}, bf16[2,1,16,320]{3,2,1,0:T(8,128)(2,1)S(1)}, u32[]{:S(2)}, u32[]{:S(2)}) collective-permute-start(bf16[2,1,16,320]{3,2,1,0:T(8,128)(2,1)S(1)} %get-tuple-element.275), channel_id=1, source_target_pairs={{1,0},{2,1},{3,2},{5,4},{6,5},{7,6},{9,8},{10,9},{11,10},{13,12},{... | collective-permute-start | bytes 61448 | tf_op jit(solution)/shard_map/ppermute | solution.py:17
  223.2 5.2 collective-permute-start.9
  230.6 5.3 collective-permute-start.11
  236.0 5.9 %collective-permute-start.13 = (bf16[2,1,16,320]{3,2,1,0:T(8,128)(2,1)S(1)}, bf16[2,1,16,320]{3,2,1,0:T(8,128)(2,1)S(1)}, u32[]{:S(2)}, u32[]{:S(2)}) collective-permute-start(bf16[2,1,16,320]{3,2,1,0:T(8,128)(2,1)S(1)} %get-tuple-element.273), channel_id=1, source_target_pairs={{1,0},{2,1},{3,2},{5,4},{6,5},{7,6},{9,8},{10,9},{11,10},{13,12},{... | collective-permute-start | bytes 61448 | tf_op jit(solution)/shard_map/ppermute | solution.py:17
  237.3 5.5 collective-permute-start.12
  243.5 1.2 copy-start.9
Sparse Core Ops, SparseCore 0:
  11.0 88.5 all-gather.2
  102.7 83.6 all-gather.4
  254.0 289.3 all-reduce.5
where the time goes:
time: 554 us; the launch traced here: 553 us
  waiting for transfers between devices  403 us (73%)
  blocking collectives  47.9 us (9%)
  starting transfers between devices  38.6 us (7%)
  local copies, waits for them, and re-layouts  37 us (7%)
  between operations  14.7 us (3%)
  matrix products  7.18 us (1%)
    unnamed x4, waiting for transfers between devices  290 us
    all_gather x1, waiting for transfers between devices, per_device(): second_all = lax.all_gather(second_convs, 'dp', axis=1, tiled=True)  66.2 us
    all_gather x1, blocking collectives, per_device(): lax.all_gather(pointwise_weights, 'dp', axis=2, tiled=True)  47.9 us
    all_gather x1, waiting for transfers between devices, per_device(): lax.all_gather(first_convs, 'dp', axis=2, tiled=True)  31.8 us
    ppermute x6, starting transfers between devices, padded_2(): lax.ppermute(lax.slice_in_dim(block, block.shape[dim] - width, None, axis...  25 us
  transfers between devices with their start and end apart: 17, of which 10 were waited for; matrix products, arithmetic and copies ran while one was open for 4% of the time, Pallas kernels for 0%

commit v1 on v0

v1 whole, which is shorter than its diff:
```python
import math

import jax
import jax.numpy as jnp
from jax import lax
from jax.experimental import pallas as pl
from jax.experimental.pallas import tpu as pltpu
from jax.sharding import PartitionSpec as P

F32 = jnp.float32
BF16 = jnp.bfloat16
C = 320
WC = 16
NX = 4
NR = 8
ROWS = 16
PAD = 3
FIRST_SLOTS = ((0, 14, 28, 42, 48), (0, 7, 21, 35, 48))
MESH = pl.DeviceIdType.MESH


def slope(value):
    logistic = 1.0 / (1.0 + jnp.exp(-value))
    return logistic * (1.0 + value * (1.0 - logistic))


def silu(value):
    return value / (1.0 + jnp.exp(-value))


def mm(left, right):
    return jnp.dot(left, right, preferred_element_type=F32)


def mm_t(left, right):
    return lax.dot_general(left, right, (((1,), (1,)), ((), ())), preferred_element_type=F32)


def flat(value):
    return value.reshape(-1, value.shape[-1])


def moved(value, by):
    count = value.shape[0]
    column = lax.broadcasted_iota(jnp.int32, value.shape, 0) & (WC - 1)
    rolled = pltpu.roll(value, by % count, 0)
    edge = 0 if by == 1 else WC - 1
    return jnp.where(column == edge, 0.0, rolled)


def conv(load, w_ref, chunk):
    parts = []
    for b in range(3):
        total = None
        for a in range(3):
            term = mm(load(a), w_ref[chunk, (3 * a + b) * C : (3 * a + b + 1) * C, :])
            total = term if total is None else total + term
        parts.append(total)
    return parts[1] + moved(parts[0], 1) + moved(parts[2], -1)


def conv_back(load, w_ref, chunk):
    parts = []
    for b in range(3):
        total = None
        for a in range(3):
            term = mm_t(load(a), w_ref[chunk, (3 * a + b) * C : (3 * a + b + 1) * C, :])
            total = term if total is None else total + term
        parts.append(total)
    return parts[1] + moved(parts[0], -1) + moved(parts[2], 1)


def inside(value, height, top):
    cell = lax.broadcasted_iota(jnp.int32, value.shape, 0)
    row = lax.rem(cell // WC, height) + top
    return jnp.where((row >= 0) & (row < ROWS), value, 0.0)


def kernel(
    lat_ref, hint_ref, dec_ref, tgt_ref, first_ref, second_ref, pwk_ref, out_ref,
    wbuf, pbuf, w_ref, pw_ref, tmp, tmp2, pwf,
    lat_all, in_all, cin_all, co_all, sg_all, fg_all,
    pre_own, act, eact, cow, cproj, skip_w, eh, dg, sgh, xsel, fgs, zs,
    slots, rsb, rsr, s2b, s2r,
    a_s, a_r, b_s, b_r, x_s, x_r, e_s, e_r, h_s, h_r, g_s, g_r,
    co_s, co_r, sg_s, sg_r, fg_s, fg_r, r1_s, r1_r, r2_s, r2_r,
):
    s = lax.axis_index("segment")
    d = lax.axis_index("dp")
    r = lax.axis_index("rows")
    zero = s == 0
    one = s == 1
    y = d // NR
    z = lax.rem(d, NR)
    pa = jnp.where(zero, z, y)
    pb = jnp.where(zero, y, z)
    own = 4 * r

    def dp_of(a, b):
        return jnp.where(zero, b * NR + a, a * NR + b)

    def ring(position, by):
        return lax.rem(position + by + NR, NR)

    def dev(a, b):
        return (s, dp_of(a, b), r)

    def row_of(k):
        return lax.rem(r + k, NX)

    def rcopy(src, dst, send, recv, device):
        return pltpu.make_async_remote_copy(
            src_ref=src, dst_ref=dst, send_sem=send, recv_sem=recv,
            device_id=device, device_id_type=MESH,
        )

    def arrived(dst, send, recv):
        rcopy(dst, dst, send, recv, (s, d, row_of(1))).wait_recv()

    for c, value in enumerate((first_ref[0, 1], first_ref[0, 0], second_ref[0])):
        wbuf[c, pb, pa, 0:45, :] = value
    pbuf[pb, pa] = pwk_ref[...]
    margin = jnp.zeros((2, PAD, WC, C), BF16)
    for ref in (lat_all, in_all, cin_all):
        ref[:, 0:PAD] = margin
        ref[:, ROWS + PAD : ROWS + 2 * PAD] = margin
    lat_all[:, pl.ds(own + PAD, 4)] = lat_ref[...]
    edge = jnp.zeros((2, 1, WC, C), BF16)
    for ref in (dg, sgh):
        ref[:, 0:1] = edge
        ref[:, 5:6] = edge

    @pl.when(zero)
    def _():
        in_all[:, pl.ds(own + PAD, 4)] = hint_ref[...]

    @pl.when(one)
    def _():
        in_all[:, pl.ds(own + PAD, 4)] = dec_ref[...]

    barrier = pltpu.get_barrier_semaphore()
    peers = [dev(ring(pa, k), pb) for k in range(1, NR)]
    peers += [dev(pa, ring(pb, k)) for k in range(1, NR)]
    for k in range(1, NX):
        peers += [(0, d, row_of(k)), (1, d, row_of(k))]
    peers += [(1 - s, d, r)]
    for peer in peers:
        pl.semaphore_signal(barrier, inc=1, device_id=peer, device_id_type=MESH)
    pl.semaphore_wait(barrier, len(peers))

    sends = []

    def stage_a(k):
        for way in range(2):
            if way and k > 3:
                continue
            sign = 1 if way == 0 else -1
            held = ring(pa, -sign * (k - 1))
            for i, (src, dst) in enumerate(
                ((pbuf.at[pb, held], pbuf.at[pb, held]), (wbuf.at[:, pb, held], wbuf.at[:, pb, held]))
            ):
                copy = rcopy(src, dst, a_s.at[i, way, k - 1], a_r.at[i, way, k - 1], dev(ring(pa, sign), pb))
                copy.start()
                sends.append(copy)

    def wait_a(k):
        for way in range(2):
            if way and k > 3:
                continue
            sign = 1 if way == 0 else -1
            got = ring(pa, -sign * k)
            arrived(pbuf.at[pb, got], a_s.at[0, way, k - 1], a_r.at[0, way, k - 1])
            arrived(wbuf.at[:, pb, got], a_s.at[1, way, k - 1], a_r.at[1, way, k - 1])

    def b_block(c, block, way, k):
        part = pl.ds(0, NR) if k < 4 else pl.ds(4 * way, 4)
        return pbuf.at[block, part] if c == 3 else wbuf.at[c, block, part]

    def stage_b(c, k):
        for way in range(2):
            sign = 1 if way == 0 else -1
            ref = b_block(c, ring(pb, -sign * (k - 1)), way, k)
            copy = rcopy(ref, ref, b_s.at[c, way, k - 1], b_r.at[c, way, k - 1], dev(pa, ring(pb, sign)))
            copy.start()
            sends.append(copy)

    def wait_b(c, k):
        for way in range(2):
            sign = 1 if way == 0 else -1
            ref = b_block(c, ring(pb, -sign * k), way, k)
            arrived(ref, b_s.at[c, way, k - 1], b_r.at[c, way, k - 1])

    stage_a(1)
    for i, ref in enumerate((lat_all, in_all)):
        for k in range(1, NX):
            mine = ref.at[:, pl.ds(own + PAD, 4)]
            copy = rcopy(mine, mine, x_s.at[i, k], x_r.at[i, k], (s, d, row_of(k)))
            copy.start()
            sends.append(copy)
    for k in range(2, 5):
        wait_a(k - 1)
        stage_a(k)
    wait_a(4)
    for c in (3, 0, 1):
        stage_b(c, 1)
    for c in (3, 0, 1):
        wait_b(c, 1)
        stage_b(c, 2)
    stage_b(2, 1)
    for c in (3, 0, 1):
        wait_b(c, 2)
        stage_b(c, 3)
    wait_b(2, 1)
    stage_b(2, 2)
    for c in (3, 0, 1):
        wait_b(c, 3)
        stage_b(c, 4)
    wait_b(2, 2)
    stage_b(2, 3)
    for i, ref in enumerate((lat_all, in_all)):
        for k in range(1, NX):
            theirs = ref.at[:, pl.ds(4 * row_of(NX - k) + PAD, 4)]
            arrived(theirs, x_s.at[i, k], x_r.at[i, k])

    def compact(c):
        @pl.loop(0, 4)
        def _(g):
            for j in range(16):
                index = g * 16 + j
                hi, lo = index // NR, lax.rem(index, NR)
                block = wbuf[c, jnp.where(zero, hi, lo), jnp.where(zero, lo, hi)]
                tmp[45 * j : 45 * j + 48, :] = block.astype(F32)
            w_ref[c, pl.ds(pl.multiple_of(g * 720, 16), 720), :] = tmp[0:720, :].astype(BF16)

    def compact_points():
        @pl.loop(0, NR)
        def _(g):
            for k in range(2):
                for j in range(NR):
                    block = pbuf[jnp.where(zero, g, j), jnp.where(zero, j, g)]
                    tmp2[k, 5 * j : 5 * j + 8, :] = block.astype(F32)[8 * k : 8 * k + 8]
                pwf[k, pl.ds(pl.multiple_of(g * 40, 8), 40), :] = tmp2[k, 0:40, :]
        pw_ref[...] = pwf[...].astype(BF16)

    other = (1 - s, d, r)

    wait_b(3, 4)
    compact_points()

    @pl.when(zero)
    def _():
        mixed = mm(flat(in_all[:, PAD : ROWS + PAD]), pw_ref[0])
        mixed = mixed + flat(lat_all[:, PAD : ROWS + PAD]).astype(F32)
        cin_all[:, PAD : ROWS + PAD] = mixed.astype(BF16).reshape(2, ROWS, WC, C)
        body = cin_all.at[:, PAD : ROWS + PAD]
        rcopy(body, body, e_s.at[0], e_r.at[0], other).start()

    wait_b(0, 4)
    compact(0)

    @pl.when(zero)
    def _():
        pre = conv(lambda a: flat(cin_all[:, pl.ds(own + a, 8)]), w_ref, 0)
        kept = pre.reshape(2, 8, WC, C)
        pre_own[...] = kept[:, 2:6]
        act[...] = inside(silu(pre), 8, own - 2).astype(BF16).reshape(2, 8, WC, C)

    @pl.when(one)
    def _():
        pre = conv(lambda a: flat(in_all[:, pl.ds(own + PAD - 1 + a, 4)]), w_ref, 0)
        pre_own[...] = pre.reshape(2, 4, WC, C)

    wait_b(2, 3)
    stage_b(2, 4)
    wait_b(1, 4)
    compact(1)

    @pl.when(zero)
    def _():
        pre = conv(lambda a: flat(lat_all[:, pl.ds(own + a, 8)]), w_ref, 1)
        eact[...] = inside(silu(pre), 8, own - 2).astype(BF16).reshape(2, 8, WC, C)
        rcopy(eact, eact, e_s.at[1], e_r.at[1], other).start()

    wait_b(2, 4)
    compact(2)

    def select_first():
        for tap in range(5):
            line = jnp.where(zero, tap // 3, (4 + tap) // 3)
            start = jnp.where(zero, FIRST_SLOTS[0][tap], FIRST_SLOTS[1][tap])
            m = lax.broadcasted_iota(jnp.int32, (128, C), 0)
            c = lax.broadcasted_iota(jnp.int32, (128, C), 1)
            row = ((180 * (start + (m >> 3)) + 45 * r) >> 3) + (m & 7) - (C * tap - 160 * s)
            pick = jnp.where((c == row) & ((m & 7) < 7), 1.0, 0.0).astype(BF16)
            held = flat(cin_all[:, pl.ds(line + PAD - 1, ROWS)])
            xsel[tap] = mm_t(pick, held).astype(BF16)

    def spread(ref, send, recv):
        copies = []
        mine = ref.at[:, pl.ds(own, 4)]
        for k in range(1, NX):
            for core in range(2):
                copies.append(rcopy(mine, mine, send.at[k, core], recv.at[k], (core, d, row_of(k))))
        copies.append(rcopy(mine, mine, send.at[0, 0], recv.at[0], other))
        return copies

    def gathered(ref, send, recv, source):
        for k in range(1, NX):
            arrived(ref.at[:, pl.ds(4 * row_of(NX - k), 4)], send.at[k, 0], recv.at[k])

        @pl.when(s != source)
        def _():
            arrived(ref.at[:, pl.ds(own, 4)], send.at[0, 0], recv.at[0])

    @pl.when(zero)
    def _():
        total = conv(lambda a: flat(act[:, a : a + 6]), w_ref, 2)
        total = total + flat(cin_all[:, pl.ds(own + PAD - 1, 6)]).astype(F32)
        out = total.astype(BF16)
        cow[...] = out.reshape(2, 6, WC, C)
        cproj[...] = mm(out, pw_ref[1]).astype(BF16).reshape(2, 6, WC, C)
        rcopy(cproj, cproj, e_s.at[2], e_r.at[2], other).start()
        co_all[:, pl.ds(own, 4)] = cow[:, 1:5]
        for copy in spread(co_all, co_s, co_r):
            copy.start()
        select_first()

    def to_halo(k):
        src = dg.at[:, 1:2] if k < 0 else dg.at[:, 4:5]
        dst = dg.at[:, 5:6] if k < 0 else dg.at[:, 0:1]
        i = 0 if k < 0 else 1
        return rcopy(src, dst, h_s.at[i], h_r.at[i], (s, d, r + k))

    def to_control(k):
        mine = pl.ds(own, 4) if k == 0 else pl.ds(own, 1) if k < 0 else pl.ds(own + 3, 1)
        dst = sgh.at[:, 1:5] if k == 0 else sgh.at[:, 5:6] if k < 0 else sgh.at[:, 0:1]
        return rcopy(sg_all.at[:, mine], dst, g_s.at[k + 1], g_r.at[k + 1], (0, d, r + k))

    @pl.when(one)
    def _():
        arrived(eact, e_s.at[1], e_r.at[1])
        total = conv(lambda a: flat(eact[:, a : a + 6]), w_ref, 1)
        total = total + flat(lat_all[:, pl.ds(own + PAD - 1, 6)]).astype(F32)
        arrived(cproj, e_s.at[2], e_r.at[2])
        total = total + flat(cproj[...]).astype(F32)
        skip = inside(total, 6, own - 1).astype(BF16)
        skip_w[...] = skip.reshape(2, 6, WC, C)
        pre = flat(pre_own[...]) + conv(lambda a: flat(skip_w[:, a : a + 4]), w_ref, 2)
        output = silu(pre) + mm(flat(in_all[:, pl.ds(own + PAD, 4)]), pw_ref[0])
        output = output + mm(flat(skip_w[:, 1:5]), pw_ref[1])
        error = (output - flat(tgt_ref[...]).astype(F32)) * (1.0 / math.sqrt(128 * ROWS * WC))
        eh[...] = error.astype(BF16)
        dg[:, 1:5] = (error * slope(pre)).astype(BF16).reshape(2, 4, WC, C)
        for k in (-1, 1):
            @pl.when((r + k >= 0) & (r + k < NX))
            def _():
                to_halo(k).start()

        @pl.when(r < NX - 1)
        def _():
            arrived(dg.at[:, 5:6], h_s.at[0], h_r.at[0])

        @pl.when(r > 0)
        def _():
            arrived(dg.at[:, 0:1], h_s.at[1], h_r.at[1])

        back = conv_back(lambda a: flat(dg[:, 2 - a : 6 - a]), w_ref, 2)
        back = back + mm_t(eh[...], pw_ref[1])
        sg_all[:, pl.ds(own, 4)] = back.astype(BF16).reshape(2, 4, WC, C)
        to_control(0).start()
        for k in (-1, 1):
            @pl.when((r + k >= 0) & (r + k < NX))
            def _():
                to_control(k).start()
        for copy in spread(sg_all, sg_s, sg_r):
            copy.start()
        arrived(cin_all.at[:, PAD : ROWS + PAD], e_s.at[0], e_r.at[0])
        select_first()

    @pl.when(zero)
    def _():
        arrived(sgh.at[:, 1:5], g_s.at[1], g_r.at[1])

        @pl.when(r < NX - 1)
        def _():
            arrived(sgh.at[:, 5:6], g_s.at[0], g_r.at[0])

        @pl.when(r > 0)
        def _():
            arrived(sgh.at[:, 0:1], g_s.at[2], g_r.at[2])

        act[:, 0:6] = mm_t(flat(sgh[...]), pw_ref[1]).astype(BF16).reshape(2, 6, WC, C)
        back = conv_back(lambda a: flat(act[:, 2 - a : 6 - a]), w_ref, 2)
        grad = back * slope(flat(pre_own[...]))
        fg_all[:, pl.ds(own, 4)] = grad.astype(BF16).reshape(2, 4, WC, C)
        for copy in spread(fg_all, fg_s, fg_r):
            copy.start()

    gathered(co_all, co_s, co_r, 0)
    gathered(sg_all, sg_s, sg_r, 1)
    m = lax.broadcasted_iota(jnp.int32, (128, C), 0)
    c = lax.broadcasted_iota(jnp.int32, (128, C), 1)
    row = 160 * s + ((20 * (m & 63) + 5 * r) >> 3) + (m >> 6)
    pick = jnp.where(c == row, 1.0, 0.0).astype(BF16)
    picked = mm_t(pick, flat(co_all[...])).astype(BF16)
    both = mm(picked, flat(sg_all[...]))
    m = lax.broadcasted_iota(jnp.int32, (64, C), 0)
    lane = lax.broadcasted_iota(jnp.int32, (64, C), 1)
    zs[...] = jnp.where(lane >= 40 * ((4 * m + 5 * r) & 7), both[0:64], both[64:128])
    slots[...] = jnp.zeros(slots.shape, F32)
    for i in range(64):
        slots[i, 7:8, :] = zs[i : i + 1, :]

    gathered(fg_all, fg_s, fg_r, 0)
    whole = flat(fg_all[...])
    wide = whole.astype(F32)
    fgs[1] = whole
    fgs[0] = moved(wide, -1).astype(BF16)
    fgs[2] = moved(wide, 1).astype(BF16)
    for tap in range(5):
        column = jnp.where(zero, tap % 3, (4 + tap) % 3)
        start = jnp.where(zero, FIRST_SLOTS[0][tap], FIRST_SLOTS[1][tap])
        block = mm(xsel[tap], fgs[column])
        slots[pl.ds(start, 16)] += block.reshape(16, NR, C)

    @pl.when(zero)
    def _():
        for a in range(NR):
            part = jnp.concatenate([slots[NR * b + a] for b in range(NR)], axis=0)
            rsb[a] = part.astype(BF16)

    @pl.when(one)
    def _():
        for a in range(NR):
            part = jnp.concatenate([slots[NR * a + b] for b in range(NR)], axis=0)
            rsb[a] = part.astype(BF16)

    for k in range(1, NR):
        to = ring(pa, k)
        copy = rcopy(rsb.at[to], rsr.at[k], r1_s.at[k], r1_r.at[k], dev(to, pb))
        copy.start()
        sends.append(copy)
    total = rsb[pa].astype(F32)
    for k in range(1, NR):
        arrived(rsr.at[k], r1_s.at[k], r1_r.at[k])
        total = total + rsr[k].astype(F32)
    s2b[...] = total.reshape(NR, NR, C)
    for k in range(1, NR):
        to = ring(pb, k)
        copy = rcopy(s2b.at[to], s2r.at[k], r2_s.at[k], r2_r.at[k], dev(pa, to))
        copy.start()
        sends.append(copy)
    total = s2b[pb]
    for k in range(1, NR):
        arrived(s2r.at[k], r2_s.at[k], r2_r.at[k])
        total = total + s2r[k]
    out_ref[...] = total

    for copy in sends:
        copy.wait_send()

    @pl.when(zero)
    def _():
        body = cin_all.at[:, PAD : ROWS + PAD]
        for i, ref in enumerate((body, eact, cproj)):
            rcopy(ref, ref, e_s.at[i], e_r.at[i], other).wait_send()
        for copy in spread(co_all, co_s, co_r) + spread(fg_all, fg_s, fg_r):
            copy.wait_send()

    @pl.when(one)
    def _():
        to_control(0).wait_send()
        for k in (-1, 1):
            @pl.when((r + k >= 0) & (r + k < NX))
            def _():
                to_halo(k).wait_send()
                to_control(k).wait_send()
        for copy in spread(sg_all, sg_s, sg_r):
            copy.wait_send()


def per_device(latent, hint, decoder_in, target, first_convs, second_convs, pointwise):
    pwk = jnp.pad(pointwise[0], ((0, 0), (0, 3), (0, 0))).reshape(16, C)
    full = (2, ROWS, WC, C)
    padded = (2, ROWS + 2 * PAD, WC, C)
    vm = pltpu.VMEM
    dma = pltpu.SemaphoreType.DMA
    scratch = [
        vm((3, NR, NR, 48, C), BF16), vm((NR, NR, 16, C), BF16), vm((3, 9 * C, C), BF16),
        vm((2, C, C), BF16), vm((728, C), F32), vm((2, 48, C), F32), vm((2, C, C), F32),
        vm(padded, BF16), vm(padded, BF16), vm(padded, BF16), vm(full, BF16), vm(full, BF16), vm(full, BF16),
        vm((2, 4, WC, C), F32), vm((2, 8, WC, C), BF16), vm((2, 8, WC, C), BF16), vm((2, 6, WC, C), BF16),
        vm((2, 6, WC, C), BF16), vm((2, 6, WC, C), BF16), vm((128, C), BF16), vm((2, 6, WC, C), BF16),
        vm((2, 6, WC, C), BF16), vm((5, 128, 512), BF16), vm((3, 512, C), BF16), vm((64, C), F32),
        vm((64, NR, C), F32), vm((NR, 64, C), BF16), vm((NR, 64, C), BF16), vm((NR, NR, C), F32), vm((NR, NR, C), F32),
        dma((2, 2, 4)), dma((2, 2, 4)), dma((4, 2, 4)), dma((4, 2, 4)), dma((2, 4)), dma((2, 4)),
        dma((3,)), dma((3,)), dma((2,)), dma((2,)), dma((3,)), dma((3,)),
        dma((4, 2)), dma((4,)), dma((4, 2)), dma((4,)), dma((4, 2)), dma((4,)),
        dma((NR,)), dma((NR,)), dma((NR,)), dma((NR,)),
    ]
    got = pl.pallas_call(
        kernel,
        out_shape=jax.ShapeDtypeStruct((8, C), F32),
        in_specs=[pl.BlockSpec(memory_space=pltpu.VMEM)] * 7,
        out_specs=pl.BlockSpec(memory_space=pltpu.VMEM),
        scratch_shapes=scratch,
        compiler_params=pltpu.CompilerParams(
            collective_id=0, has_side_effects=True, vmem_limit_bytes=56 * 1024 * 1024
        ),
        name="step",
    )(latent, hint, decoder_in, target, first_convs, second_convs, pwk)
    d = lax.axis_index("dp")
    r = lax.axis_index("rows")
    offset = 40 * ((4 * d + 5 * r) & 7)
    first = lax.dynamic_slice(got[:7].reshape(-1), (offset,), (1800,))
    last = got[7]
    second = lax.dynamic_slice(jnp.concatenate([last, last]), (offset,), (200,))
    return first, second


def solution(mesh):
    placed = (
        P("dp", "rows", None, None),
        P("dp", "rows", None, None),
        P("dp", "rows", None, None),
        P("dp", "rows", None, None),
        P("segment", None, "dp", None),
        P("segment", "dp", None),
        P("segment", None, "dp", None),
    )
    return jax.shard_map(
        per_device,
        mesh=mesh,
        in_specs=placed,
        out_specs=(P(("segment", "dp", "rows")), P(("segment", "dp", "rows"))),
        check_vma=False,
    )
```

time: 554 us -> 119 us (0.21)
  waiting for transfers between devices: 403 us -> 0 us
  Pallas kernels: 0 us -> 113 us
  blocking collectives: 47.9 us -> 0 us
  starting transfers between devices: 38.6 us -> 0 us
  local copies, waits for them, and re-layouts: 37 us -> 4.95 us
  between operations: 14.7 us -> 0.65 us
  matrix products: 7.18 us -> 0 us
    unnamed x4 -> x0, waiting for transfers between devices: 290 us -> none
    pallas_call x0 -> x1, Pallas kernels: none -> 113 us  [per_device(): pl.pallas_call(kernel, out_shape=jax.ShapeDtypeStruct((8, C), F32), in_sp...]
    all_gather x2 -> x0, waiting for transfers between devices: 98 us -> none  [the longest x1 66.2 us: per_device(): second_all = lax.all_gather(second_convs, 'dp', axis=1, tiled=True)]
    all_gather x1 -> x0, blocking collectives: 47.9 us -> none  [per_device(): lax.all_gather(pointwise_weights, 'dp', axis=2, tiled=True)]
    ppermute x14 -> x0, starting transfers between devices: 38.5 us -> none  [the longest x6 25 us: padded_2(): lax.ppermute(lax.slice_in_dim(block, block.shape[dim] - width, None, axis...]
    ppermute x14 -> x0, waiting for transfers between devices: 15 us -> none  [the longest x2 7.88 us: shifted(): return lax.ppermute(array, axis, pairs)]
    slice x9 -> x1, local copies, waits for them, and re-layouts: 11.7 us -> 0.72 us  [per_device(): last = got[7]]
    unnamed x40 -> x4, local copies, waits for them, and re-layouts: 10.6 us -> 1.53 us
  transfers between devices with their start and end apart: 17 -> 0, of which waited for: 10 -> 0; matrix products, arithmetic and copies ran while one was open for 4% -> 0% of each run, Pallas kernels for 0% -> 0%
where the time goes in v1:
time: 119 us
  Pallas kernels  113 us (95%)
  local copies, waits for them, and re-layouts  4.95 us (4%)
    pallas_call x1, Pallas kernels, per_device(): pl.pallas_call(kernel, out_shape=jax.ShapeDtypeStruct((8, C), F32), in_sp...  113 us

profile of v1, /device:TPU:1, one launch (start us, length us, event | category | flops | bytes accessed | tf_op | source)
XLA Modules:
  0.0 119.1 jit_solution(9807302194351722193)
XLA Ops:
  0.6 0.0 copy-start
  0.6 1.5 %copy.10.first_ref = bf16[1,2,45,320]{3,2,1,0:T(8,128)(2,1)} copy(bf16[1,2,45,320]{3,1,2,0:T(2,128)(2,1)} %param.11) | data formatting | bytes 115200 | tf_op args[4]
  2.2 0.0 copy-done
  2.2 0.6 pad_bitcast_fusion.pwk_ref
  2.8 113.4 %step.1 = f32[8,320]{1,0:T(8,128)} custom-call(bf16[2,4,16,320]{3,2,1,0:T(8,128)(2,1)} %lat_ref.1, bf16[2,4,16,320]{3,2,1,0:T(8,128)(2,1)} %hint_ref.1, bf16[2,4,16,320]{3,2,1,0:T(8,128)(2,1)} %dec_ref.1, bf16[2,4,16,320]{3,2,1,0:T(8,128)(2,1)} %tgt_ref.1, bf16[1,2,45,320]{3,2,1,0:T(8,128)(2,1)} %copy.10.first_ref, bf16[1,45,320]{2,1,0:T(8,128)(2,1)} %second_ref.1, ...), custom_call_target="tpu_custom_call" | custom-call | tf_op jit(solution)/shard_map/step/pallas_call | solution.py:501
  116.2 0.8 reshape.11
  117.0 0.7 dynamic_slice.6
  117.6 0.7 slice_reduce_fusion
  118.4 0.1 pad_maximum_fusion
  118.4 0.6 dynamic_slice.7
  (1 shorter events, 0.0 us)
Async XLA Ops:
  0.6 1.5 %copy-start = (bf16[1,2,5,320]{3,1,2,0:T(2,128)(2,1)S(1)}, bf16[1,2,5,320]{3,1,2,0:T(2,128)(2,1)}, u32[]{:S(2)}) copy-start(bf16[1,2,5,320]{3,1,2,0:T(2,128)(2,1)} %param.13) | copy-start | bytes 19204

commit v2 on v0

v2 whole, which is shorter than its diff:
```python
import math

import jax
import jax.numpy as jnp
from jax import lax
from jax.experimental import pallas as pl
from jax.experimental.pallas import tpu as pltpu
from jax.sharding import PartitionSpec as P

F32 = jnp.float32
BF16 = jnp.bfloat16
C = 320
WC = 16
NX = 4
NR = 8
ROWS = 16
CELLS = ROWS * WC
HEIGHTS = (64, 48, 48)
ALONE = (2, 2, 2)
FIRST_SLOTS = ((0, 14, 28, 42, 48), (0, 7, 21, 35, 48))
MESH = pl.DeviceIdType.MESH


def slope(value):
    logistic = 1.0 / (1.0 + jnp.exp(-value))
    return logistic * (1.0 + value * (1.0 - logistic))


def silu(value):
    return value / (1.0 + jnp.exp(-value))


def mm(left, right):
    return jnp.dot(left, right, preferred_element_type=F32)


def mm_t(left, right):
    return lax.dot_general(left, right, (((1,), (1,)), ((), ())), preferred_element_type=F32)


def flat(value):
    return value.reshape(-1, value.shape[-1])


def moved(value, by):
    count = value.shape[0]
    column = lax.broadcasted_iota(jnp.int32, value.shape, 0) & (WC - 1)
    rolled = pltpu.roll(value, by % count, 0)
    edge = 0 if by == 1 else WC - 1
    return jnp.where(column == edge, 0.0, rolled)


def taps(load, w_ref, segment, chunk, product):
    parts = []
    for b in range(3):
        total = None
        for a in range(3):
            term = product(load(a), w_ref[segment, chunk, (3 * a + b) * C : (3 * a + b + 1) * C, :])
            total = term if total is None else total + term
        parts.append(total)
    return parts


def conv(ref, w_ref, segment, chunk):
    parts = taps(lambda a: flat(ref[a : a + ROWS]), w_ref, segment, chunk, mm)
    return parts[1] + moved(parts[0], 1) + moved(parts[2], -1)


def conv_back(ref, w_ref, segment, chunk):
    parts = taps(lambda a: flat(ref[2 - a : 2 - a + ROWS]), w_ref, segment, chunk, mm_t)
    return parts[1] + moved(parts[0], -1) + moved(parts[2], 1)


def place(by):
    if by == 0:
        return 0
    return 7 if abs(by) == 4 else 2 * by if by > 0 else -2 * by - 1


def kernel(
    lat_ref, hint_ref, dec_ref, tgt_ref, first_ref, second_ref, pwk_ref, out_ref,
    buf0, buf1, buf2, w_ref, pw_ref, tmp, tmp2, pwf,
    xin, cin2, co2, sg2, fg2, pre_c, pre_d, base, act, eact, skip_p, dg, xsel, fgs, zs,
    slots, rsb, rsr, s2b, s2r,
    a_s, a_r, b_s, b_r, x_s, x_r, d_s, d_r, i_s, i_r, e_s, e_r, r1_s, r1_r, r2_s, r2_r,
):
    s = lax.axis_index("segment")
    d = lax.axis_index("dp")
    r = lax.axis_index("rows")
    zero = s == 0
    y = d // NR
    z = lax.rem(d, NR)
    pa = jnp.where(zero, z, y)
    pb = jnp.where(zero, y, z)
    odd = lax.rem(r, 2)
    own = 4 * r
    bufs = (buf0, buf1, buf2)

    def ring(position, by):
        return lax.rem(position + by + NR, NR)

    def dev(by_a, by_b):
        a, b = ring(pa, by_a), ring(pb, by_b)
        return (s, jnp.where(zero, b * NR + a, a * NR + b), r)

    def row_of(k):
        return lax.rem(r + k + NX, NX)

    other = (1 - s, d, r)
    sends = []

    def rcopy(src, dst, send, recv, device):
        return pltpu.make_async_remote_copy(
            src_ref=src, dst_ref=dst, send_sem=send, recv_sem=recv,
            device_id=device, device_id_type=MESH,
        )

    def push(src, dst, send, recv, device):
        copy = rcopy(src, dst, send, recv, device)
        copy.start()
        sends.append(copy)

    def arrived(dst, send, recv):
        rcopy(dst, dst, send, recv, other).wait_recv()

    buf0[0, 0, 0, 0:45, :] = first_ref[0, 1]
    buf0[0, 0, 0, 48:64, :] = pwk_ref[...]
    buf1[0, 0, 0, 0:45, :] = first_ref[0, 0]
    buf2[0, 0, 0, 0:45, :] = second_ref[0]
    edge = jnp.zeros((1, WC, C), BF16)
    for ref in [xin.at[0], xin.at[2], cin2.at[0], cin2.at[1], act, eact, skip_p, dg]:
        ref[0:1] = edge
        ref[ROWS + 1 : ROWS + 2] = edge
    for i, ref in enumerate((lat_ref, hint_ref, dec_ref, tgt_ref)):
        xin[i, pl.ds(own + 1, 4)] = ref[s]

    barrier = pltpu.get_barrier_semaphore()
    peers = [dev(k, 0) for k in range(1, NR)] + [dev(0, k) for k in range(1, NR)]
    peers += [(s, d, row_of(k)) for k in range(1, NX)] + [other]
    for peer in peers:
        pl.semaphore_signal(barrier, inc=1, device_id=peer, device_id_type=MESH)
    pl.semaphore_wait(barrier, len(peers))

    def a_part(c, k, way):
        return bufs[c].at[0, 0, place(k if way else -k)]

    def send_a(c, k):
        for way in range(2 if k < 4 else 1):
            push(a_part(c, k - 1, way), a_part(c, k, way), a_s.at[c, way, k - 1], a_r.at[c, way, k - 1], dev(-1 if way else 1, 0))

    def wait_a(c, k):
        for way in range(2 if k < 4 else 1):
            arrived(a_part(c, k, way), a_s.at[c, way, k - 1], a_r.at[c, way, k - 1])

    def mine(c):
        return pl.ds(ALONE[c] * odd, ALONE[c])

    def theirs(c):
        return pl.ds(ALONE[c] * (1 - odd), ALONE[c])

    def both(c):
        return pl.ds(2 * ALONE[c], NR - 2 * ALONE[c])

    def ways(part, k):
        return (0, 1) if k < 4 else (part,)

    def b_part(c, part, k, way):
        which = mine(c) if part else both(c)
        return bufs[c].at[0, place(k if way else -k), which]

    def send_b(c, part, k):
        for way in ways(part, k):
            push(
                b_part(c, part, k - 1, way), b_part(c, part, k, way),
                b_s.at[c, part, way, k - 1], b_r.at[c, part, way, k - 1], dev(0, -1 if way else 1),
            )

    def wait_b(c, part, k):
        for way in ways(part, k):
            arrived(b_part(c, part, k, way), b_s.at[c, part, way, k - 1], b_r.at[c, part, way, k - 1])

    def send_x(c, k):
        for way in ways(1, k):
            ref = b_part(c, 1, k, way)
            push(ref, ref, x_s.at[c, way, k - 1], x_r.at[c, way, k - 1], (s, d, row_of(-1 if way else 1)))

    def wait_x(c, k):
        for way in ways(1, k):
            ref = bufs[c].at[0, place(k if way else -k), theirs(c)]
            arrived(ref, x_s.at[c, way, k - 1], x_r.at[c, way, k - 1])

    def span(k):
        return pl.ds(0, 1) if k == 0 else pl.ds(7, 1) if k == 4 else pl.ds(2 * k - 1, 2)

    def send_d(c, k):
        push(bufs[c].at[0, span(k)], bufs[c].at[1, span(k)], d_s.at[c, k], d_r.at[c, k], other)

    def wait_d(c):
        for k in range(5):
            arrived(bufs[c].at[1, span(k)], d_s.at[c, k], d_r.at[c, k])

    def turn(i, c):
        if i == 0:
            send_a(c, 1)
        elif i == 1:
            wait_a(c, 1)
            send_a(c, 2)
        elif i == 2:
            wait_a(c, 2)
            send_a(c, 3)
            send_b(c, 1, 1)
        elif i == 3:
            wait_a(c, 3)
            send_a(c, 4)
            wait_b(c, 1, 1)
            send_b(c, 1, 2)
            send_x(c, 1)
        elif i == 4:
            wait_a(c, 4)
            send_b(c, 0, 1)
            send_d(c, 0)
        elif i in (5, 7, 9):
            k = (i - 1) // 2
            wait_b(c, 1, k)
            if k < 4:
                send_b(c, 1, k + 1)
            send_x(c, k)
        elif i in (6, 8, 10):
            k = (i - 4) // 2
            wait_b(c, 0, k)
            send_b(c, 0, k + 1)
            wait_x(c, k)
            send_d(c, k)
        elif i == 11:
            wait_b(c, 0, 4)
            wait_x(c, 4)
            send_d(c, 4)

    for c in range(3):
        turn(0, c)
    part = xin.at[:, pl.ds(own + 1, 4)]
    for k in range(1, NX):
        push(part, part, i_s.at[k], i_r.at[k], (s, d, row_of(k)))
    lag = 3
    for i in range(1, 12):
        if i == 4:
            pass
        if i == 8:
            pass
        for c in (0, 1):
            turn(i, c)
        if 0 < i - lag:
            turn(i - lag, 2)

    def compact(c, segment):
        held = jnp.where(s == segment, 0, 1)

        @pl.loop(0, 4)
        def _(g):
            for j in range(16):
                yy, zz = 2 * g + j // NR, j % NR
                a, b = ((zz, yy), (yy, zz))[segment]
                at_a, at_b = ((z, y), (y, z))[segment]
                block = bufs[c][held, spot(b - at_b), spot(a - at_a), 0:48]
                tmp[45 * j : 45 * j + 48, :] = block.astype(F32)
            w_ref[segment, c, pl.ds(pl.multiple_of(g * 720, 16), 720), :] = tmp[0:720, :].astype(BF16)

    def spot(by):
        by = lax.rem(by + NR, NR)
        return jnp.where(by < 4, 2 * by, 15 - 2 * by)

    def compact_points(segment):
        held = jnp.where(s == segment, 0, 1)

        @pl.loop(0, NR)
        def _(g):
            for k in range(2):
                for j in range(NR):
                    a, b = ((j, g), (g, j))[segment]
                    at_a, at_b = ((z, y), (y, z))[segment]
                    block = buf0[held, spot(b - at_b), spot(a - at_a), 48:64]
                    tmp2[k, 5 * j : 5 * j + 8, :] = block.astype(F32)[8 * k : 8 * k + 8]
                pwf[k, pl.ds(pl.multiple_of(g * 40, 8), 40), :] = tmp2[k, 0:40, :]
        pw_ref[segment] = pwf[...].astype(BF16)

    def store(ref, value):
        ref[1 : ROWS + 1] = value.astype(BF16).reshape(ROWS, WC, C)

    def inner(ref):
        return flat(ref[1 : ROWS + 1])

    def swap(ref, i):
        push(ref.at[s], ref.at[s], e_s.at[i], e_r.at[i], other)

    def swapped(ref, i):
        arrived(ref.at[1 - s], e_s.at[i], e_r.at[i])

    for k in range(1, NX):
        arrived(xin.at[:, pl.ds(4 * row_of(-k) + 1, 4)], i_s.at[k], i_r.at[k])
    lat, hint, dec, tgt = xin.at[0], xin.at[1], xin.at[2], xin.at[3]
    wait_d(0)
    for segment in range(2):
        compact_points(segment)
        compact(0, segment)
    own_in = cin2.at[s]
    store(own_in, mm(inner(hint), pw_ref[0, 0]) + inner(lat).astype(F32))
    swap(cin2, 0)
    pre = conv(own_in, w_ref, 0, 0)
    pre_c[...] = pre
    store(act, silu(pre))
    pre_d[...] = conv(dec, w_ref, 1, 0)
    turn(9, 2)
    wait_d(1)
    for segment in range(2):
        compact(1, segment)
    store(eact, silu(conv(lat, w_ref, 0, 1)))
    turn(10, 2)
    base[...] = conv(eact, w_ref, 1, 1) + inner(lat).astype(F32)
    turn(11, 2)
    wait_d(2)
    for segment in range(2):
        compact(2, segment)
    out = (conv(act, w_ref, 0, 2) + inner(own_in).astype(F32)).astype(BF16)
    co2[s] = out
    swap(co2, 1)
    proj = mm(out, pw_ref[0, 1]).astype(BF16)
    store(skip_p, base[...] + proj.astype(F32))
    pre = pre_d[...] + conv(skip_p, w_ref, 1, 2)
    output = silu(pre) + mm(inner(dec), pw_ref[1, 0]) + mm(inner(skip_p), pw_ref[1, 1])
    error = (output - inner(tgt).astype(F32)) * (1.0 / math.sqrt(128 * ROWS * WC))
    store(dg, error * slope(pre))
    back = conv_back(dg, w_ref, 1, 2) + mm_t(error.astype(BF16), pw_ref[1, 1])
    sg = back.astype(BF16)
    sg2[s] = sg
    swap(sg2, 2)
    store(act, mm_t(sg, pw_ref[0, 1]))
    grad = conv_back(act, w_ref, 0, 2) * slope(pre_c[...])
    fg2[s] = grad.astype(BF16)
    swap(fg2, 3)

    swapped(cin2, 0)
    swapped(co2, 1)
    swapped(sg2, 2)
    for tap in range(5):
        line = jnp.where(zero, tap // 3, (4 + tap) // 3)
        start = jnp.where(zero, FIRST_SLOTS[0][tap], FIRST_SLOTS[1][tap])
        m = lax.broadcasted_iota(jnp.int32, (128, C), 0)
        c = lax.broadcasted_iota(jnp.int32, (128, C), 1)
        row = ((180 * (start + (m >> 3)) + 45 * r) >> 3) + (m & 7) - (C * tap - 160 * s)
        pick = jnp.where((c == row) & ((m & 7) < 7), 1.0, 0.0).astype(BF16)
        held = flat(cin2[:, pl.ds(line, ROWS)])
        xsel[tap] = mm_t(pick, held).astype(BF16)
    m = lax.broadcasted_iota(jnp.int32, (128, C), 0)
    c = lax.broadcasted_iota(jnp.int32, (128, C), 1)
    row = 160 * s + ((20 * (m & 63) + 5 * r) >> 3) + (m >> 6)
    pick = jnp.where(c == row, 1.0, 0.0).astype(BF16)
    picked = mm_t(pick, flat(co2[...])).astype(BF16)
    pair = mm(picked, flat(sg2[...]))
    m = lax.broadcasted_iota(jnp.int32, (64, C), 0)
    lane = lax.broadcasted_iota(jnp.int32, (64, C), 1)
    zs[...] = jnp.where(lane >= 40 * ((4 * m + 5 * r) & 7), pair[0:64], pair[64:128])
    slots[...] = jnp.zeros(slots.shape, F32)
    for i in range(64):
        slots[i, 7:8, :] = zs[i : i + 1, :]

    swapped(fg2, 3)
    whole = flat(fg2[...])
    wide = whole.astype(F32)
    fgs[1] = whole
    fgs[0] = moved(wide, -1).astype(BF16)
    fgs[2] = moved(wide, 1).astype(BF16)
    for tap in range(5):
        column = jnp.where(zero, tap % 3, (4 + tap) % 3)
        start = jnp.where(zero, FIRST_SLOTS[0][tap], FIRST_SLOTS[1][tap])
        slots[pl.ds(start, 16)] += mm(xsel[tap], fgs[column]).reshape(16, NR, C)

    @pl.when(zero)
    def _():
        for a in range(NR):
            rsb[a] = jnp.concatenate([slots[NR * b + a] for b in range(NR)], axis=0).astype(BF16)

    @pl.when(s == 1)
    def _():
        for a in range(NR):
            rsb[a] = jnp.concatenate([slots[NR * a + b] for b in range(NR)], axis=0).astype(BF16)

    for k in range(1, NR):
        push(rsb.at[ring(pa, k)], rsr.at[k], r1_s.at[k], r1_r.at[k], dev(k, 0))
    total = rsb[pa].astype(F32)
    for k in range(1, NR):
        arrived(rsr.at[k], r1_s.at[k], r1_r.at[k])
        total = total + rsr[k].astype(F32)
    s2b[...] = total.reshape(NR, NR, C)
    for k in range(1, NR):
        push(s2b.at[ring(pb, k)], s2r.at[k], r2_s.at[k], r2_r.at[k], dev(0, k))
    total = s2b[pb]
    for k in range(1, NR):
        arrived(s2r.at[k], r2_s.at[k], r2_r.at[k])
        total = total + s2r[k]
    out_ref[...] = total
    for copy in sends:
        copy.wait_send()


def per_device(latent, hint, decoder_in, target, first_convs, second_convs, pointwise):
    pwk = jnp.pad(pointwise[0], ((0, 0), (0, 3), (0, 0))).reshape(16, C)
    vm = pltpu.VMEM
    dma = pltpu.SemaphoreType.DMA
    image = (ROWS + 2, WC, C)
    cells = (CELLS, C)
    scratch = [vm((2, NR, NR, height, C), BF16) for height in HEIGHTS]
    scratch += [
        vm((2, 3, 9 * C, C), BF16), vm((2, 2, C, C), BF16), vm((728, C), F32), vm((2, 48, C), F32), vm((2, C, C), F32),
        vm((4,) + image, BF16), vm((2,) + image, BF16), vm((2,) + cells, BF16), vm((2,) + cells, BF16),
        vm((2,) + cells, BF16), vm(cells, F32), vm(cells, F32), vm(cells, F32),
        vm(image, BF16), vm(image, BF16), vm(image, BF16), vm(image, BF16),
        vm((5, 128, 2 * CELLS), BF16), vm((3, 2 * CELLS, C), BF16), vm((64, C), F32),
        vm((64, NR, C), F32), vm((NR, 64, C), BF16), vm((NR, 64, C), BF16), vm((NR, NR, C), F32), vm((NR, NR, C), F32),
    ]
    for shape in ((3, 2, 4), (3, 2, 2, 4), (3, 2, 4), (3, 5), (4,), (4,), (NR,), (NR,)):
        scratch += [dma(shape), dma(shape)]
    got = pl.pallas_call(
        kernel,
        out_shape=jax.ShapeDtypeStruct((8, C), F32),
        in_specs=[pl.BlockSpec(memory_space=pltpu.VMEM)] * 7,
        out_specs=pl.BlockSpec(memory_space=pltpu.VMEM),
        scratch_shapes=scratch,
        compiler_params=pltpu.CompilerParams(
            collective_id=0, has_side_effects=True, vmem_limit_bytes=60 * 1024 * 1024
        ),
        name="step",
    )(latent, hint, decoder_in, target, first_convs, second_convs, pwk)
    d = lax.axis_index("dp")
    r = lax.axis_index("rows")
    offset = 40 * ((4 * d + 5 * r) & 7)
    first = lax.dynamic_slice(got[:7].reshape(-1), (offset,), (1800,))
    last = got[7]
    second = lax.dynamic_slice(jnp.concatenate([last, last]), (offset,), (200,))
    return first, second


def solution(mesh):
    placed = (
        P("dp", "rows", None, None),
        P("dp", "rows", None, None),
        P("dp", "rows", None, None),
        P("dp", "rows", None, None),
        P("segment", None, "dp", None),
        P("segment", "dp", None),
        P("segment", None, "dp", None),
    )
    return jax.shard_map(
        per_device,
        mesh=mesh,
        in_specs=placed,
        out_specs=(P(("segment", "dp", "rows")), P(("segment", "dp", "rows"))),
        check_vma=False,
    )
```

time: 554 us -> 103 us (0.19)
  waiting for transfers between devices: 403 us -> 0 us
  Pallas kernels: 0 us -> 95.6 us
  blocking collectives: 47.9 us -> 0 us
  starting transfers between devices: 38.6 us -> 0 us
  local copies, waits for them, and re-layouts: 37 us -> 4.95 us
  between operations: 14.7 us -> 0.65 us
  matrix products: 7.18 us -> 0 us
    unnamed x4 -> x0, waiting for transfers between devices: 290 us -> none
    all_gather x2 -> x0, waiting for transfers between devices: 98 us -> none  [the longest x1 66.2 us: per_device(): second_all = lax.all_gather(second_convs, 'dp', axis=1, tiled=True)]
    pallas_call x0 -> x1, Pallas kernels: none -> 95.6 us  [per_device(): pl.pallas_call(kernel, out_shape=jax.ShapeDtypeStruct((8, C), F32), in_sp...]
    all_gather x1 -> x0, blocking collectives: 47.9 us -> none  [per_device(): lax.all_gather(pointwise_weights, 'dp', axis=2, tiled=True)]
    ppermute x14 -> x0, starting transfers between devices: 38.5 us -> none  [the longest x6 25 us: padded_2(): lax.ppermute(lax.slice_in_dim(block, block.shape[dim] - width, None, axis...]
    ppermute x14 -> x0, waiting for transfers between devices: 15 us -> none  [the longest x2 7.88 us: shifted(): return lax.ppermute(array, axis, pairs)]
    slice x9 -> x1, local copies, waits for them, and re-layouts: 11.7 us -> 0.72 us  [per_device(): last = got[7]]
    unnamed x40 -> x4, local copies, waits for them, and re-layouts: 10.6 us -> 1.53 us
  transfers between devices with their start and end apart: 17 -> 0, of which waited for: 10 -> 0; matrix products, arithmetic and copies ran while one was open for 4% -> 0% of each run, Pallas kernels for 0% -> 0%
where the time goes in v2:
time: 103 us; the launch traced here: 101 us
  Pallas kernels  95.6 us (93%)
  local copies, waits for them, and re-layouts  4.95 us (5%)
    pallas_call x1, Pallas kernels, per_device(): pl.pallas_call(kernel, out_shape=jax.ShapeDtypeStruct((8, C), F32), in_sp...  95.6 us

profile of v2, /device:TPU:1, one launch (start us, length us, event | category | flops | bytes accessed | tf_op | source)
XLA Modules:
  0.0 101.3 jit_solution(4015803214082946976)
XLA Ops:
  0.6 0.0 copy-start
  0.6 1.5 %copy.10.first_ref = bf16[1,2,45,320]{3,2,1,0:T(8,128)(2,1)} copy(bf16[1,2,45,320]{3,1,2,0:T(2,128)(2,1)} %param.11) | data formatting | bytes 115200 | tf_op args[4]
  2.2 0.0 copy-done
  2.2 0.6 pad_bitcast_fusion.pwk_ref
  2.8 95.6 %step.1 = f32[8,320]{1,0:T(8,128)} custom-call(bf16[2,4,16,320]{3,2,1,0:T(8,128)(2,1)} %lat_ref.1, bf16[2,4,16,320]{3,2,1,0:T(8,128)(2,1)} %hint_ref.1, bf16[2,4,16,320]{3,2,1,0:T(8,128)(2,1)} %dec_ref.1, bf16[2,4,16,320]{3,2,1,0:T(8,128)(2,1)} %tgt_ref.1, bf16[1,2,45,320]{3,2,1,0:T(8,128)(2,1)} %copy.10.first_ref, bf16[1,45,320]{2,1,0:T(8,128)(2,1)} %second_ref.1, ...), custom_call_target="tpu_custom_call" | custom-call | tf_op jit(solution)/shard_map/step/pallas_call | solution.py:422
  98.4 0.8 reshape.11
  99.2 0.7 dynamic_slice.6
  99.9 0.7 slice_reduce_fusion
  100.6 0.1 pad_maximum_fusion
  100.7 0.6 dynamic_slice.7
  (1 shorter events, 0.0 us)
Async XLA Ops:
  0.6 1.5 %copy-start = (bf16[1,2,5,320]{3,1,2,0:T(2,128)(2,1)S(1)}, bf16[1,2,5,320]{3,1,2,0:T(2,128)(2,1)}, u32[]{:S(2)}) copy-start(bf16[1,2,5,320]{3,1,2,0:T(2,128)(2,1)} %param.13) | copy-start | bytes 19204

commit v3 on v2

--- a/solution.py
+++ b/solution.py
@@ -15,7 +15,10 @@
 NR = 8
 ROWS = 16
 CELLS = ROWS * WC
-HEIGHTS = (64, 48, 48)
+BLOCKS = ((32, 640), (48, 384), (48, 256))
+WIDE = 384
+LAGS = (0, 1, 3)
+FAR = (4, 3, 5, 2, 6, 1, 7)
 ALONE = (2, 2, 2)
 FIRST_SLOTS = ((0, 14, 28, 42, 48), (0, 7, 21, 35, 48))
 MESH = pl.DeviceIdType.MESH
@@ -78,11 +81,11 @@
 
 
 def kernel(
-    lat_ref, hint_ref, dec_ref, tgt_ref, first_ref, second_ref, pwk_ref, out_ref,
+    lat_ref, hint_ref, dec_ref, tgt_ref, first_ref, second_ref, points_ref, out_ref,
     buf0, buf1, buf2, w_ref, pw_ref, tmp, tmp2, pwf,
-    xin, cin2, co2, sg2, fg2, pre_c, pre_d, base, act, eact, skip_p, dg, xsel, fgs, zs,
+    pack, xin, cin2, co2, sg2, fg2, pre_c, pre_d, base, act, eact, skip_p, dg, xsel, fgs, zs,
     slots, rsb, rsr, s2b, s2r,
-    a_s, a_r, b_s, b_r, x_s, x_r, d_s, d_r, i_s, i_r, e_s, e_r, r1_s, r1_r, r2_s, r2_r,
+    a_s, a_r, b_s, b_r, x_s, x_r, d_s, d_r, i_s, i_r, e_s, e_r, r1_s, r1_r, r2_s, r2_r, l_s,
 ):
     s = lax.axis_index("segment")
     d = lax.axis_index("dp")
@@ -123,17 +126,34 @@
     def arrived(dst, send, recv):
         rcopy(dst, dst, send, recv, other).wait_recv()
 
-    buf0[0, 0, 0, 0:45, :] = first_ref[0, 1]
-    buf0[0, 0, 0, 48:64, :] = pwk_ref[...]
-    buf1[0, 0, 0, 0:45, :] = first_ref[0, 0]
-    buf2[0, 0, 0, 0:45, :] = second_ref[0]
+    inputs = [
+        pltpu.make_async_copy(ref.at[s], xin.at[i, pl.ds(own + 1, 4)], l_s.at[i])
+        for i, ref in enumerate((lat_ref, hint_ref, dec_ref, tgt_ref))
+    ]
+
+    def joined(left, right):
+        lane = lax.broadcasted_iota(jnp.int32, (left.shape[0], 128), 1)
+        return jnp.where(lane < 64, left[:, 256:384], pltpu.roll(right[:, 256:384], 64, 1)).astype(BF16)
+
+    for copy in inputs:
+        copy.start()
+    pack[...] = jnp.zeros(pack.shape, F32)
+    pack[0, 0:45, 0:C] = first_ref[:, 1, :].astype(F32)
+    pack[1, 0:45, 0:C] = first_ref[:, 0, :].astype(F32)
+    pack[2, 0:45, 0:C] = second_ref[0].astype(F32)
+    pack[0, 48:53, 0:C] = points_ref[:, 0, :].astype(F32)
+    pack[0, 56:61, 0:C] = points_ref[:, 1, :].astype(F32)
+    low, high = pack[0, 0:32], pack[0, 32:64]
+    buf0[0, 0, 0, :, 0:256] = low[:, 0:256].astype(BF16)
+    buf0[0, 0, 0, :, 256:512] = high[:, 0:256].astype(BF16)
+    buf0[0, 0, 0, :, 512:640] = joined(low, high)
+    buf1[0, 0, 0, :, 0:256] = pack[1, 0:48, 0:256].astype(BF16)
+    buf1[0, 0, 0, :, 256:384] = joined(pack[1, 0:48], pack[2, 0:48])
+    buf2[0, 0, 0] = pack[2, 0:48, 0:256].astype(BF16)
     edge = jnp.zeros((1, WC, C), BF16)
     for ref in [xin.at[0], xin.at[2], cin2.at[0], cin2.at[1], act, eact, skip_p, dg]:
         ref[0:1] = edge
         ref[ROWS + 1 : ROWS + 2] = edge
-    for i, ref in enumerate((lat_ref, hint_ref, dec_ref, tgt_ref)):
-        xin[i, pl.ds(own + 1, 4)] = ref[s]
-
     barrier = pltpu.get_barrier_semaphore()
     peers = [dev(k, 0) for k in range(1, NR)] + [dev(0, k) for k in range(1, NR)]
     peers += [(s, d, row_of(k)) for k in range(1, NX)] + [other]
@@ -225,61 +245,90 @@
             if k < 4:
                 send_b(c, 1, k + 1)
             send_x(c, k)
+            if i > 5:
+                send_xd(c, k - 2)
         elif i in (6, 8, 10):
             k = (i - 4) // 2
             wait_b(c, 0, k)
             send_b(c, 0, k + 1)
-            wait_x(c, k)
-            send_d(c, k)
         elif i == 11:
+            send_xd(c, 3)
             wait_b(c, 0, 4)
-            wait_x(c, 4)
-            send_d(c, 4)
+            send_xd(c, 4)
+
+    def send_xd(c, k):
+        wait_x(c, k)
+        send_d(c, k)
 
     for c in range(3):
         turn(0, c)
-    part = xin.at[:, pl.ds(own + 1, 4)]
-    for k in range(1, NX):
-        push(part, part, i_s.at[k], i_r.at[k], (s, d, row_of(k)))
-    lag = 3
+    for copy in inputs:
+        copy.wait()
+
+    def rows_of(k, half=None):
+        which = pl.ds(0, 4) if half is None else pl.ds(2 * half, 2)
+        return xin.at[which, pl.ds(4 * row_of(k) + 1, 4)]
+
+    for i, k in enumerate((1, -1)):
+        push(rows_of(0), rows_of(0), i_s.at[0, i], i_r.at[0, i], (s, d, row_of(k)))
     for i in range(1, 12):
-        if i == 4:
-            pass
-        if i == 8:
-            pass
-        for c in (0, 1):
-            turn(i, c)
-        if 0 < i - lag:
-            turn(i - lag, 2)
-
-    def compact(c, segment):
-        held = jnp.where(s == segment, 0, 1)
+        turn(i, 0)
+        for c in (1, 2):
+            if i < 4:
+                turn(i, c)
+            elif i - LAGS[c] > 3:
+                turn(i - LAGS[c], c)
+        if i == 3:
+            for at, k in enumerate((1, -1)):
+                arrived(rows_of(-k), i_s.at[0, at], i_r.at[0, at])
+                ref = rows_of(-k, at)
+                push(ref, ref, i_s.at[1, at], i_r.at[1, at], (s, d, row_of(k)))
+
+    def spot(by):
+        by = lax.rem(by + NR, NR)
+        return jnp.where(by < 4, 2 * by, 15 - 2 * by)
+
+    def spots(segment, yy, zz):
+        first = segment == 0
+        at_y, at_z = spot(yy - y), spot(zz - z)
+        return jnp.where(first, at_y, at_z), jnp.where(first, at_z, at_y)
+
+    def tail(block):
+        return pltpu.roll(block, 64, 1)[:, 0:64]
+
+    def compact(c, held):
+        segment = jnp.where(held == 0, s, 1 - s)
 
         @pl.loop(0, 4)
         def _(g):
             for j in range(16):
-                yy, zz = 2 * g + j // NR, j % NR
-                a, b = ((zz, yy), (yy, zz))[segment]
-                at_a, at_b = ((z, y), (y, z))[segment]
-                block = bufs[c][held, spot(b - at_b), spot(a - at_a), 0:48]
-                tmp[45 * j : 45 * j + 48, :] = block.astype(F32)
+                at = (held,) + spots(segment, 2 * g + j // NR, j % NR)
+                row = 45 * j
+                if c == 0:
+                    low, high = buf0[at], buf0[at + (slice(0, 16),)]
+                    tmp[row : row + 32, 0:256] = low[:, 0:256].astype(F32)
+                    tmp[row : row + 32, 256:C] = low[:, 512:576].astype(F32)
+                    tmp[row + 32 : row + 48, 0:256] = high[:, 256:512].astype(F32)
+                    tmp[row + 32 : row + 48, 256:C] = tail(high[:, 512:640].astype(F32))
+                elif c == 1:
+                    tmp[row : row + 48, :] = buf1[at][:, 0:C].astype(F32)
+                else:
+                    tmp[row : row + 48, 0:256] = buf2[at].astype(F32)
+                    tmp[row : row + 48, 256:C] = tail(buf1[at][:, 256:384].astype(F32))
             w_ref[segment, c, pl.ds(pl.multiple_of(g * 720, 16), 720), :] = tmp[0:720, :].astype(BF16)
 
-    def spot(by):
-        by = lax.rem(by + NR, NR)
-        return jnp.where(by < 4, 2 * by, 15 - 2 * by)
-
-    def compact_points(segment):
-        held = jnp.where(s == segment, 0, 1)
+    def compact_points(held):
+        segment = jnp.where(held == 0, s, 1 - s)
 
         @pl.loop(0, NR)
         def _(g):
+            for j in range(NR):
+                block = buf0[(held,) + spots(segment, g, j) + (slice(16, 32),)]
+                main, last = block[:, 256:512].astype(F32), tail(block[:, 512:640].astype(F32))
+                for k in range(2):
+                    tmp2[k, 5 * j : 5 * j + 8, 0:256] = main[8 * k : 8 * k + 8]
+                    tmp2[k, 5 * j : 5 * j + 8, 256:C] = last[8 * k : 8 * k + 8]
             for k in range(2):
-                for j in range(NR):
-                    a, b = ((j, g), (g, j))[segment]
-                    at_a, at_b = ((z, y), (y, z))[segment]
-                    block = buf0[held, spot(b - at_b), spot(a - at_a), 48:64]
-                    tmp2[k, 5 * j : 5 * j + 8, :] = block.astype(F32)[8 * k : 8 * k + 8]
                 pwf[k, pl.ds(pl.multiple_of(g * 40, 8), 40), :] = tmp2[k, 0:40, :]
         pw_ref[segment] = pwf[...].astype(BF16)
 
@@ -295,31 +344,43 @@
     def swapped(ref, i):
         arrived(ref.at[1 - s], e_s.at[i], e_r.at[i])
 
-    for k in range(1, NX):
-        arrived(xin.at[:, pl.ds(4 * row_of(-k) + 1, 4)], i_s.at[k], i_r.at[k])
+    for i in range(2):
+        arrived(rows_of(2, i), i_s.at[1, i], i_r.at[1, i])
     lat, hint, dec, tgt = xin.at[0], xin.at[1], xin.at[2], xin.at[3]
+    compact_points(0)
+    compact(0, 0)
+    turn(11, 1)
+    turn(9, 2)
     wait_d(0)
-    for segment in range(2):
-        compact_points(segment)
-        compact(0, segment)
+    compact_points(1)
+    compact(0, 1)
+    turn(10, 2)
     own_in = cin2.at[s]
     store(own_in, mm(inner(hint), pw_ref[0, 0]) + inner(lat).astype(F32))
     swap(cin2, 0)
     pre = conv(own_in, w_ref, 0, 0)
     pre_c[...] = pre
     store(act, silu(pre))
+    compact(1, 0)
     pre_d[...] = conv(dec, w_ref, 1, 0)
-    turn(9, 2)
+    turn(11, 2)
     wait_d(1)
-    for segment in range(2):
-        compact(1, segment)
+    compact(1, 1)
     store(eact, silu(conv(lat, w_ref, 0, 1)))
-    turn(10, 2)
     base[...] = conv(eact, w_ref, 1, 1) + inner(lat).astype(F32)
-    turn(11, 2)
+    compact(2, 0)
+    swapped(cin2, 0)
+    for tap in range(5):
+        line = jnp.where(zero, tap // 3, (4 + tap) // 3)
+        start = jnp.where(zero, FIRST_SLOTS[0][tap], FIRST_SLOTS[1][tap])
+        m = lax.broadcasted_iota(jnp.int32, (128, C), 0)
+        c = lax.broadcasted_iota(jnp.int32, (128, C), 1)
+        row = ((180 * (start + (m >> 3)) + 45 * r) >> 3) + (m & 7) - (C * tap - 160 * s)
+        pick = jnp.where((c == row) & ((m & 7) < 7), 1.0, 0.0).astype(BF16)
+        held = flat(cin2[:, pl.ds(line, ROWS)])
+        xsel[tap] = mm_t(pick, held).astype(BF16)
     wait_d(2)
-    for segment in range(2):
-        compact(2, segment)
+    compact(2, 1)
     out = (conv(act, w_ref, 0, 2) + inner(own_in).astype(F32)).astype(BF16)
     co2[s] = out
     swap(co2, 1)
@@ -338,18 +399,8 @@
     fg2[s] = grad.astype(BF16)
     swap(fg2, 3)
 
-    swapped(cin2, 0)
     swapped(co2, 1)
     swapped(sg2, 2)
-    for tap in range(5):
-        line = jnp.where(zero, tap // 3, (4 + tap) // 3)
-        start = jnp.where(zero, FIRST_SLOTS[0][tap], FIRST_SLOTS[1][tap])
-        m = lax.broadcasted_iota(jnp.int32, (128, C), 0)
-        c = lax.broadcasted_iota(jnp.int32, (128, C), 1)
-        row = ((180 * (start + (m >> 3)) + 45 * r) >> 3) + (m & 7) - (C * tap - 160 * s)
-        pick = jnp.where((c == row) & ((m & 7) < 7), 1.0, 0.0).astype(BF16)
-        held = flat(cin2[:, pl.ds(line, ROWS)])
-        xsel[tap] = mm_t(pick, held).astype(BF16)
     m = lax.broadcasted_iota(jnp.int32, (128, C), 0)
     c = lax.broadcasted_iota(jnp.int32, (128, C), 1)
     row = 160 * s + ((20 * (m & 63) + 5 * r) >> 3) + (m >> 6)
@@ -384,59 +435,58 @@
         for a in range(NR):
             rsb[a] = jnp.concatenate([slots[NR * a + b] for b in range(NR)], axis=0).astype(BF16)
 
-    for k in range(1, NR):
+    for k in FAR:
         push(rsb.at[ring(pa, k)], rsr.at[k], r1_s.at[k], r1_r.at[k], dev(k, 0))
     total = rsb[pa].astype(F32)
     for k in range(1, NR):
         arrived(rsr.at[k], r1_s.at[k], r1_r.at[k])
         total = total + rsr[k].astype(F32)
     s2b[...] = total.reshape(NR, NR, C)
-    for k in range(1, NR):
+    for k in FAR:
         push(s2b.at[ring(pb, k)], s2r.at[k], r2_s.at[k], r2_r.at[k], dev(0, k))
     total = s2b[pb]
     for k in range(1, NR):
         arrived(s2r.at[k], r2_s.at[k], r2_r.at[k])
         total = total + s2r[k]
-    out_ref[...] = total
+    off = 40 * ((4 * d + 5 * r) & 7)
+    wide = jnp.concatenate([total, jnp.zeros((NR, WIDE - C), F32)], axis=1)
+    after = jnp.where(lax.broadcasted_iota(jnp.int32, wide.shape, 0) == 7, wide, pltpu.roll(wide, 7, 0))
+    lane = lax.broadcasted_iota(jnp.int32, wide.shape, 1)
+    wide = jnp.where(lane < C - off, pltpu.roll(wide, lax.rem(WIDE - off, WIDE), 1), pltpu.roll(after, C - off, 1))
+    out_ref[...] = wide[:, 0:C]
     for copy in sends:
         copy.wait_send()
 
 
 def per_device(latent, hint, decoder_in, target, first_convs, second_convs, pointwise):
-    pwk = jnp.pad(pointwise[0], ((0, 0), (0, 3), (0, 0))).reshape(16, C)
     vm = pltpu.VMEM
     dma = pltpu.SemaphoreType.DMA
     image = (ROWS + 2, WC, C)
     cells = (CELLS, C)
-    scratch = [vm((2, NR, NR, height, C), BF16) for height in HEIGHTS]
+    scratch = [vm((2, NR, NR) + block, BF16) for block in BLOCKS]
     scratch += [
         vm((2, 3, 9 * C, C), BF16), vm((2, 2, C, C), BF16), vm((728, C), F32), vm((2, 48, C), F32), vm((2, C, C), F32),
-        vm((4,) + image, BF16), vm((2,) + image, BF16), vm((2,) + cells, BF16), vm((2,) + cells, BF16),
+        vm((3, 64, WIDE), F32), vm((4,) + image, BF16), vm((2,) + image, BF16), vm((2,) + cells, BF16), vm((2,) + cells, BF16),
         vm((2,) + cells, BF16), vm(cells, F32), vm(cells, F32), vm(cells, F32),
         vm(image, BF16), vm(image, BF16), vm(image, BF16), vm(image, BF16),
         vm((5, 128, 2 * CELLS), BF16), vm((3, 2 * CELLS, C), BF16), vm((64, C), F32),
         vm((64, NR, C), F32), vm((NR, 64, C), BF16), vm((NR, 64, C), BF16), vm((NR, NR, C), F32), vm((NR, NR, C), F32),
     ]
-    for shape in ((3, 2, 4), (3, 2, 2, 4), (3, 2, 4), (3, 5), (4,), (4,), (NR,), (NR,)):
+    for shape in ((3, 2, 4), (3, 2, 2, 4), (3, 2, 4), (3, 5), (2, 2), (4,), (NR,), (NR,)):
         scratch += [dma(shape), dma(shape)]
+    scratch += [dma((4,))]
     got = pl.pallas_call(
         kernel,
         out_shape=jax.ShapeDtypeStruct((8, C), F32),
-        in_specs=[pl.BlockSpec(memory_space=pltpu.VMEM)] * 7,
+        in_specs=[pl.BlockSpec(memory_space=pl.ANY)] * 4 + [pl.BlockSpec(memory_space=pltpu.VMEM)] * 3,
         out_specs=pl.BlockSpec(memory_space=pltpu.VMEM),
         scratch_shapes=scratch,
         compiler_params=pltpu.CompilerParams(
             collective_id=0, has_side_effects=True, vmem_limit_bytes=60 * 1024 * 1024
         ),
         name="step",
-    )(latent, hint, decoder_in, target, first_convs, second_convs, pwk)
-    d = lax.axis_index("dp")
-    r = lax.axis_index("rows")
-    offset = 40 * ((4 * d + 5 * r) & 7)
-    first = lax.dynamic_slice(got[:7].reshape(-1), (offset,), (1800,))
-    last = got[7]
-    second = lax.dynamic_slice(jnp.concatenate([last, last]), (offset,), (200,))
-    return first, second
+    )(latent, hint, decoder_in, target, jnp.swapaxes(first_convs[0], 0, 1), second_convs, jnp.swapaxes(pointwise[0], 0, 1))
+    return got[:6].reshape(-1)[:1800], got[7, :200]
 
 
 def solution(mesh):

time: 103 us -> 92.6 us (0.90); the launches traced: 101 us -> 92.3 us
  Pallas kernels: 95.6 us -> 89 us
  local copies, waits for them, and re-layouts: 4.95 us -> 2.64 us
    pallas_call x1, Pallas kernels: 95.6 us -> 89 us  [per_device(): pl.pallas_call(kernel, out_shape=jax.ShapeDtypeStruct((8, C), F32), in_sp...]
    unnamed x4 -> x0, local copies, waits for them, and re-layouts: 1.53 us -> none
    dynamic_slice x2 -> x0, local copies, waits for them, and re-layouts: 1.31 us -> none  [the longest x1 0.67 us: per_device(): first = lax.dynamic_slice(got[:7].reshape(-1), (offset,), (1800,))]
where the time goes in v3:
time: 92.6 us; the launch traced here: 92.3 us
  Pallas kernels  89 us (96%)
  local copies, waits for them, and re-layouts  2.64 us (3%)
    pallas_call x1, Pallas kernels, per_device(): pl.pallas_call(kernel, out_shape=jax.ShapeDtypeStruct((8, C), F32), in_sp...  89 us

profile of v3, /device:TPU:1, one launch (start us, length us, event | category | flops | bytes accessed | tf_op | source)
XLA Modules:
  0.0 92.3 jit_solution(11680778169649866589)
XLA Ops:
  0.6 89.0 %step.1 = f32[8,320]{1,0:T(8,128)} custom-call(bf16[2,4,16,320]{3,2,1,0:T(8,128)(2,1)} %lat_ref.1, bf16[2,4,16,320]{3,2,1,0:T(8,128)(2,1)} %hint_ref.1, bf16[2,4,16,320]{3,2,1,0:T(8,128)(2,1)} %dec_ref.1, bf16[2,4,16,320]{3,2,1,0:T(8,128)(2,1)} %tgt_ref.1, bf16[45,2,320]{2,1,0:T(2,128)(2,1)} %bitcast.9, bf16[1,45,320]{2,1,0:T(8,128)(2,1)} %second_ref.1, ...), custom_call_target="tpu_custom_call" | custom-call | tf_op jit(solution)/shard_map/step/pallas_call | solution.py:478
  89.7 1.3 %slice.11 = f32[1,200]{1,0:T(1,128)} slice(f32[8,320]{1,0:T(8,128)} %step.1), slice={[7:8], [0:200]} | slice | bytes 1600 | tf_op jit(solution)/shard_map/slice | solution.py:489
  90.9 1.4 %reshape.7 = f32[1920]{0:T(1024)} reshape(f32[6,320]{1,0:T(8,128)} %bitcast.10) | data formatting | bytes 15360 | tf_op jit(solution)/shard_map/reshape | solution.py:489

commit v4 on v3

--- a/solution.py
+++ b/solution.py
@@ -155,8 +155,7 @@
         ref[0:1] = edge
         ref[ROWS + 1 : ROWS + 2] = edge
     barrier = pltpu.get_barrier_semaphore()
-    peers = [dev(k, 0) for k in range(1, NR)] + [dev(0, k) for k in range(1, NR)]
-    peers += [(s, d, row_of(k)) for k in range(1, NX)] + [other]
+    peers = [dev(1, 0), dev(-1, 0), dev(0, 1), dev(0, -1), (s, d, row_of(1)), (s, d, row_of(-1)), other]
     for peer in peers:
         pl.semaphore_signal(barrier, inc=1, device_id=peer, device_id_type=MESH)
     pl.semaphore_wait(barrier, len(peers))
@@ -349,11 +348,11 @@
     lat, hint, dec, tgt = xin.at[0], xin.at[1], xin.at[2], xin.at[3]
     compact_points(0)
     compact(0, 0)
-    turn(11, 1)
     turn(9, 2)
     wait_d(0)
     compact_points(1)
     compact(0, 1)
+    turn(11, 1)
     turn(10, 2)
     own_in = cin2.at[s]
     store(own_in, mm(inner(hint), pw_ref[0, 0]) + inner(lat).astype(F32))

time: 92.6 us -> 90.5 us (0.977)
  Pallas kernels: 89 us -> 86.9 us
    pallas_call x1, Pallas kernels: 89 us -> 86.9 us  [per_device(): pl.pallas_call(kernel, out_shape=jax.ShapeDtypeStruct((8, C), F32), in_sp...]
where the time goes in v4:
time: 90.5 us; the launch traced here: 90.2 us
  Pallas kernels  86.9 us (96%)
  local copies, waits for them, and re-layouts  2.64 us (3%)
    pallas_call x1, Pallas kernels, per_device(): pl.pallas_call(kernel, out_shape=jax.ShapeDtypeStruct((8, C), F32), in_sp...  86.9 us

profile of v4, /device:TPU:1, one launch (start us, length us, event | category | flops | bytes accessed | tf_op | source)
XLA Modules:
  0.0 90.2 jit_solution(12543710153739539060)
XLA Ops:
  0.6 86.9 %step.1 = f32[8,320]{1,0:T(8,128)} custom-call(bf16[2,4,16,320]{3,2,1,0:T(8,128)(2,1)} %lat_ref.1, bf16[2,4,16,320]{3,2,1,0:T(8,128)(2,1)} %hint_ref.1, bf16[2,4,16,320]{3,2,1,0:T(8,128)(2,1)} %dec_ref.1, bf16[2,4,16,320]{3,2,1,0:T(8,128)(2,1)} %tgt_ref.1, bf16[45,2,320]{2,1,0:T(2,128)(2,1)} %bitcast.9, bf16[1,45,320]{2,1,0:T(8,128)(2,1)} %second_ref.1, ...), custom_call_target="tpu_custom_call" | custom-call | tf_op jit(solution)/shard_map/step/pallas_call | solution.py:477
  87.5 1.3 %slice.11 = f32[1,200]{1,0:T(1,128)} slice(f32[8,320]{1,0:T(8,128)} %step.1), slice={[7:8], [0:200]} | slice | bytes 1600 | tf_op jit(solution)/shard_map/slice | solution.py:488
  88.8 1.4 %reshape.7 = f32[1920]{0:T(1024)} reshape(f32[6,320]{1,0:T(8,128)} %bitcast.10) | data formatting | bytes 15360 | tf_op jit(solution)/shard_map/reshape | solution.py:488
